TPU v7x, 32 devices: a whole 2x2x4 slice. The times are simulated.
32 devices in a mesh: group: 2 (over y), rows: 4 (over z), sec: 2 (over x), sub: 2 (over core).
Axes of the slice: x: 2, y: 2, z: 4, core: 2. Of those that a mesh axis runs over, the one named last changes fastest.
Arguments:
- row_seeds: int32 [16384], P(('group', 'rows')), parts along dimension 0, may hold values from 0 to 65520
- labels: int32 [16384], P(('group', 'rows')), parts along dimension 0, may hold values from 0 to 1
- weights: float32 [131072], P(('group', 'sec', 'sub')), parts along dimension 0, may hold values from -5 to 5
- sketch: bfloat16 [65536, 64], P(('sec', 'sub')), may hold values from -5 to 5
Outputs:
- step: float32 [131072], P(('group', 'sec', 'sub')), parts along dimension 0
- sketched: float32 [131072, 64], P(('group', 'sec', 'sub')), parts along dimension 0
There are 2 independent parts, one for each index of `group`. A program takes and returns all parts, laid end to end along the dimension named above; an argument that names none is the same for every part. Nothing has to cross between parts.
All inputs are finite; a program needn't handle non-finite values.
Results may differ from a plain program's by a relative error of at most 0.0029.
Values may be sent and summed in bfloat16 or wider, within the bound.
No kernel may reach another device: no remote copies, remote signals or barrier semaphores. Data moves between devices by JAX's collectives and lax.ppermute only.
A program may use at most 128 MiB of HBM per device.

v0:
```python
import jax
import jax.numpy as jnp
from jax import lax
from jax.sharding import PartitionSpec as P

ROOT = 256


def table_block(seeds, first, count):
    cols = first + lax.iota(jnp.int32, count)
    part_a = cols * 30011 % 65521
    part_b = seeds * 16411 % 65521
    mixer = (part_b[:, None] + part_a[None, :]) % 65521
    folded = mixer % 46337
    mixer = folded * folded % 65521
    mixer = (mixer * 31 + part_a[None, :] + 7) % 65521
    level = mixer % 16
    return ((level.astype(jnp.float32) - 7.5) * (1.0 / (4.0 * ROOT))).astype(jnp.bfloat16)


def block_size():
    return 512


def margin_rows(seeds, first, stacked):
    count = seeds.shape[0]
    blk = block_size()
    nblk = count // blk
    nfeat = stacked.shape[0]

    def one_block(block_seeds):
        return jnp.dot(
            table_block(block_seeds, first, nfeat), stacked, preferred_element_type=jnp.float32
        )

    return lax.map(one_block, seeds.reshape(nblk, blk)).reshape(count, stacked.shape[1])


def accumulate(seeds, mixed, first, nfeat):
    count = seeds.shape[0]
    blk = block_size()
    nblk = count // blk

    def add_block(index, acc):
        block_seeds = lax.dynamic_slice_in_dim(seeds, index * blk, blk, 0)
        block_mixed = lax.dynamic_slice_in_dim(mixed, index * blk, blk, 0)
        tab = table_block(block_seeds, first, nfeat)
        return acc + lax.dot_general(
            tab, block_mixed, (((0,), (0,)), ((), ())), preferred_element_type=jnp.float32
        )

    return lax.fori_loop(0, nblk, add_block, jnp.zeros((nfeat, mixed.shape[1]), jnp.float32))


def weigh(margins, labels):
    prob = jax.nn.sigmoid(margins[:, 0])
    resid = prob - labels.astype(jnp.float32)
    curv = prob * (1.0 - prob)
    return jnp.concatenate([resid[:, None], curv[:, None] * margins[:, 1:]], axis=1).astype(
        jnp.bfloat16
    )


def products(sketch_part, sketched, grad):
    highest = lax.Precision.HIGHEST
    core = lax.dot_general(
        sketch_part.astype(jnp.float32), sketched, (((0,), (0,)), ((), ())), precision=highest
    )
    square = lax.dot_general(sketched, sketched, (((0,), (0,)), ((), ())), precision=highest)
    proj = lax.dot_general(sketched, grad, (((0,), (0,)), ((), ())), precision=highest)
    return (core, square, proj)


def finish(core, square, proj, sketched, grad, lam):
    inner = lam * core + square
    inner = 0.5 * (inner + inner.T)
    factor = jnp.linalg.cholesky(inner)
    middle = lax.linalg.triangular_solve(factor, proj[:, None], left_side=True, lower=True)
    coef = lax.linalg.triangular_solve(
        factor, middle, left_side=True, lower=True, transpose_a=True
    )[:, 0]
    return (grad - jnp.dot(sketched, coef, precision=lax.Precision.HIGHEST)) / lam


def local(row_seeds, labels, weights, sketch):
    lam = 0.05
    nfeat = weights.shape[0]
    first = lax.axis_index(("sec", "sub")) * nfeat
    stacked = jnp.concatenate([weights.astype(jnp.bfloat16)[:, None], sketch], axis=1)
    local_margins = margin_rows(row_seeds, first, stacked)
    margins = lax.psum(local_margins, ("sec", "sub"))
    mixed = weigh(margins, labels)
    partial_total = accumulate(row_seeds, mixed, first, nfeat)
    piece = lax.psum_scatter(partial_total, "rows", scatter_dimension=0, tiled=True)
    count = piece.shape[0]
    position = lax.axis_index("rows") * count
    own_weights = lax.dynamic_slice_in_dim(weights, position, count, 0)
    own_sketch = lax.dynamic_slice_in_dim(sketch, position, count, 0)
    grad = piece[:, 0] + lam * own_weights
    sketched = piece[:, 1:] + lam * own_sketch.astype(jnp.float32)
    core, square, proj = products(own_sketch, sketched, grad)
    core, square, proj = lax.psum((core, square, proj), ("rows", "sec", "sub"))
    step = finish(core, square, proj, sketched, grad, lam)
    step, sketched = (
        lax.all_gather(step, "rows", axis=0, tiled=True),
        lax.all_gather(sketched, "rows", axis=0, tiled=True),
    )
    return (step, sketched)


def solution(mesh):
    placed = (
        P(("group", "rows")),
        P(("group", "rows")),
        P(("group", "sec", "sub")),
        P(("sec", "sub"), None),
    )
    return jax.shard_map(
        local,
        mesh=mesh,
        in_specs=placed,
        out_specs=(P(("group", "sec", "sub")), P(("group", "sec", "sub"), None)),
        check_vma=False,
    )
```

profile of v0, /device:TPU:0, one launch (start us, length us, event | category | flops | bytes accessed | tf_op | source)
XLA Modules:
  0.0 1060.1 jit_solution(18047026899343946793)
XLA Ops:
  7.2 0.0 all-reduce.3.cloned.1.call-start
  7.2 0.8 convert_element_type.47
  8.1 3.8 broadcast_in_dim.39
  11.9 4.7 copy.29
  16.7 0.7 reshape.76
  17.4 5.9 pad_maximum_fusion
  23.3 415.5 %while.30 = (s32[]{:T(128)}, f32[4,512,65]{1,0,2:T(4,128)S(1)}, s32[4,512]{1,0:T(4,128)S(1)}, s32[]{:T(128)}, bf16[16384,65]{1,0:T(8,128)(2,1)}, /*index=5*/s32[]{:T(128)}, s32[]{:T(128)}) while((s32[]{:T(128)}, f32[4,512,65]{1,0,2:T(4,128)S(1)}, s32[4,512]{1,0:T(4,128)S(1)}, s32[]{:T(128)}, bf16[16384,65]{1,0:T(8,128)(2,1)}, ...), condition=%wide.region_1.2_spmd, body=%wide.region_0.1_spmd.sunk | while | flops 1459752448 | bytes 45011060 | solution.py:36
  23.4 91.7 %fusion.121 = bf16[512,16384]{1,0:T(8,128)(2,1)} fusion(s32[16384]{0:T(1024)S(1)} %add_select_fusion.18, s32[512]{0:T(512)S(1)} %add_select_fusion.19), kind=kLoop, calls=%fused_computation.18.clone.clone.clone.clone.1.clone.1 | loop fusion | flops 369098752 | bytes 16844800 | tf_op jit(solution)/shard_map/while/body/eval_jaxpr/dot_general | solution.py:32
  115.0 8.8 fusion.122
  123.9 0.1 copy.44
  124.0 3.1 dynamic_update_slice.9
  127.3 91.7 %fusion.121 = bf16[512,16384]{1,0:T(8,128)(2,1)} fusion(s32[16384]{0:T(1024)S(1)} %add_select_fusion.18, s32[512]{0:T(512)S(1)} %add_select_fusion.19), kind=kLoop, calls=%fused_computation.18.clone.clone.clone.clone.1.clone.1 | loop fusion | flops 369098752 | bytes 16844800 | tf_op jit(solution)/shard_map/while/body/eval_jaxpr/dot_general | solution.py:32
  218.9 8.8 fusion.122
  227.7 0.1 copy.44
  227.9 3.1 dynamic_update_slice.9
  231.1 91.7 %fusion.121 = bf16[512,16384]{1,0:T(8,128)(2,1)} fusion(s32[16384]{0:T(1024)S(1)} %add_select_fusion.18, s32[512]{0:T(512)S(1)} %add_select_fusion.19), kind=kLoop, calls=%fused_computation.18.clone.clone.clone.clone.1.clone.1 | loop fusion | flops 369098752 | bytes 16844800 | tf_op jit(solution)/shard_map/while/body/eval_jaxpr/dot_general | solution.py:32
  322.8 8.8 fusion.122
  331.6 0.1 copy.44
  331.8 3.1 dynamic_update_slice.9
  335.0 91.7 %fusion.121 = bf16[512,16384]{1,0:T(8,128)(2,1)} fusion(s32[16384]{0:T(1024)S(1)} %add_select_fusion.18, s32[512]{0:T(512)S(1)} %add_select_fusion.19), kind=kLoop, calls=%fused_computation.18.clone.clone.clone.clone.1.clone.1 | loop fusion | flops 369098752 | bytes 16844800 | tf_op jit(solution)/shard_map/while/body/eval_jaxpr/dot_general | solution.py:32
  426.7 8.8 fusion.122
  435.5 0.1 copy.44
  435.7 3.1 dynamic_update_slice.9
  438.8 0.1 pad.4
  438.9 1.0 copy.42
  439.9 0.0 all-reduce.3.cloned.1.call-update
  440.0 0.0 reduce-scatter.2.cloned.1.call-start
  440.0 36.3 %all-reduce.3.cloned.1.call-done = f32[2048,65]{0,1:T(8,128)} async-done(((f32[2048,65]{0,1:T(8,128)}), f32[2048,65]{0,1:T(8,128)}) %all-reduce.3.cloned.1.call-update) | async-done | bytes 532496 | tf_op jit(solution)/shard_map/psum | solution.py:91
  476.3 0.9 subtract_multiply_fusion.1
  477.2 1.1 fusion.77
  478.3 0.1 pad_maximum_fusion.1
  478.4 0.0 copy-start.1
  478.4 381.5 %while.31 = (s32[]{:T(128)}, f32[16384,65]{0,1:T(8,128)}, s32[2048]{0:T(1024)}, s32[]{:T(128)}, bf16[2048,65]{0,1:T(8,128)(2,1)S(1)}, /*index=5*/s32[]{:T(128)}, s32[]{:T(128)}, s32[]{:T(128)}, s32[]{:T(128)}) while((s32[]{:T(128)}, f32[16384,65]{0,1:T(8,128)}, s32[2048]{0:T(1024)}, s32[]{:T(128)}, bf16[2048,65]{0,1:T(8,128)(2,1)S(1)}, ...), condition=%wide.region_4.5_spmd.clone, body=%wide.region_3.4_spmd.clone.sunk | while | flops 1461882368 | bytes 8730785 | solution.py:52
  478.6 0.9 add_select_fusion.21
  479.6 93.6 %convolution_add_fusion.2 = f32[16384,65]{0,1:T(8,128)} fusion(s32[16384]{0:T(1024)S(1)} %add_select_fusion.20, s32[512]{0:T(512)S(1)} %add_select_fusion.21, f32[16384,65]{0,1:T(8,128)} %get-tuple-element.400, pred[]{:T(512)S(6)} %compare.19, bf16[2048,65]{0,1:T(8,128)(2,1)S(1)} %get-tuple-element.412, s32[]{:T(128)S(6)} %select_n.397), kind=kOutput, calls=%fused_computation.70.clone.3 | convolution fusion | flops 1461747712 | bytes 8660997 | tf_op jit(solution)/shard_map/while/body/eval_jaxpr/dot_general | solution.py:48
  573.1 0.8 add_select_fusion.21
  574.0 94.8 %convolution_add_fusion.2 = f32[16384,65]{0,1:T(8,128)} fusion(s32[16384]{0:T(1024)S(1)} %add_select_fusion.20, s32[512]{0:T(512)S(1)} %add_select_fusion.21, f32[16384,65]{0,1:T(8,128)} %get-tuple-element.400, pred[]{:T(512)S(6)} %compare.19, bf16[2048,65]{0,1:T(8,128)(2,1)S(1)} %get-tuple-element.412, s32[]{:T(128)S(6)} %select_n.397), kind=kOutput, calls=%fused_computation.70.clone.3 | convolution fusion | flops 1461747712 | bytes 8660997 | tf_op jit(solution)/shard_map/while/body/eval_jaxpr/dot_general | solution.py:48
  668.7 0.8 add_select_fusion.21
  669.6 94.8 %convolution_add_fusion.2 = f32[16384,65]{0,1:T(8,128)} fusion(s32[16384]{0:T(1024)S(1)} %add_select_fusion.20, s32[512]{0:T(512)S(1)} %add_select_fusion.21, f32[16384,65]{0,1:T(8,128)} %get-tuple-element.400, pred[]{:T(512)S(6)} %compare.19, bf16[2048,65]{0,1:T(8,128)(2,1)S(1)} %get-tuple-element.412, s32[]{:T(128)S(6)} %select_n.397), kind=kOutput, calls=%fused_computation.70.clone.3 | convolution fusion | flops 1461747712 | bytes 8660997 | tf_op jit(solution)/shard_map/while/body/eval_jaxpr/dot_general | solution.py:48
  764.3 0.8 add_select_fusion.21
  765.2 94.8 %convolution_add_fusion.2 = f32[16384,65]{0,1:T(8,128)} fusion(s32[16384]{0:T(1024)S(1)} %add_select_fusion.20, s32[512]{0:T(512)S(1)} %add_select_fusion.21, f32[16384,65]{0,1:T(8,128)} %get-tuple-element.400, pred[]{:T(512)S(6)} %compare.19, bf16[2048,65]{0,1:T(8,128)(2,1)S(1)} %get-tuple-element.412, s32[]{:T(128)S(6)} %select_n.397), kind=kOutput, calls=%fused_computation.70.clone.3 | convolution fusion | flops 1461747712 | bytes 8660997 | tf_op jit(solution)/shard_map/while/body/eval_jaxpr/dot_general | solution.py:48
  859.9 0.0 reduce-scatter.2.cloned.1.call-update
  860.0 0.0 all-gather.2.cloned.1.call-start
  860.0 85.3 %reduce-scatter.2.cloned.1.call-done = f32[4096,65]{0,1:T(8,128)} async-done(((f32[16384,65]{0,1:T(8,128)}), f32[4096,65]{0,1:T(8,128)}) %reduce-scatter.2.cloned.1.call-update) | async-done | bytes 1064976 | tf_op jit(solution)/shard_map/reduce_scatter | solution.py:94
  945.4 2.4 slice_add_fusion
  947.8 0.0 all-gather.2.cloned.1.call-update
  947.8 0.9 slice.32
  948.7 0.7 multiply_add_fusion.1
  949.4 2.2 convolution_bitcast_fusion
  951.6 1.8 fusion.78
  953.4 2.6 fusion.91
  956.0 64.8 %all-reduce = (f32[64,64]{0,1:T(8,128)S(1)}, f32[64,64]{0,1:T(8,128)S(1)}, f32[64]{0:T(128)S(1)}) all-reduce(f32[64,64]{0,1:T(8,128)S(1)} %fusion.91, f32[64,64]{0,1:T(8,128)S(1)} %fusion.78, f32[64]{0:T(128)S(1)} %convolution_bitcast_fusion), channel_id=1, replica_groups=mesh['group'=2,'rows'=4,'sec'=2,'sub'=2] {'rows','sec','sub'}, use_global_device_ids=true, to_apply=%region_7.8 | all-reduce | flops 8256 | bytes 66048 | tf_op jit(solution)/shard_map/psum | solution.py:102
  1020.8 0.1 copy.34
  1020.9 0.1 copy.35
  1021.0 5.8 cholesky.16
  1026.9 0.6 compare_reduce_fusion
  1027.6 0.7 fusion.80
  1028.2 4.9 custom-call.8
  1033.1 0.2 convolution_bitcast_fusion.2
  1033.3 0.2 convolution_bitcast_fusion.1
  1033.4 1.9 fusion.92
  1035.3 13.1 %all_gather.6 = f32[16384]{0:T(1024)S(1)} all-gather(f32[4096]{0:T(1024)S(1)} %subtract_multiply_fusion), channel_id=1, replica_groups=mesh['group'=2,'rows'=4,'sec'=2,'sub'=2] {'rows'}, dimensions={0}, use_global_device_ids=true | all-gather | bytes 81920 | tf_op jit(solution)/shard_map/all_gather | solution.py:105
  1048.5 0.6 copy.61
  1049.1 4.5 copy.62
  (37 shorter events, 0.5 us)
Async XLA Ops:
  7.2 469.1 %all-reduce.3.cloned.1.call-start = ((), (), s32[]{:S(2)}) async-start(), calls=%async_computation.1 | async-start | bytes 1179648 | tf_op jit(solution)/shard_map/psum | solution.py:91
  23.3 453.9 %copy-start.2 = (s32[2048]{0:T(1024)S(1)}, s32[2048]{0:T(1024)}, u32[]{:S(2)}) copy-start(s32[2048]{0:T(1024)} %param.9) | copy-start | bytes 24580
  23.3 91.7 %copy-start = (bf16[16384,65]{1,0:T(8,128)(2,1)S(1)}, bf16[16384,65]{1,0:T(8,128)(2,1)}, u32[]{:S(2)}) copy-start(bf16[16384,65]{1,0:T(8,128)(2,1)} %get-tuple-element.387) | copy-start | bytes 6389764 | tf_op jit(solution)/shard_map/while
  127.2 91.8 %copy-start = (bf16[16384,65]{1,0:T(8,128)(2,1)S(1)}, bf16[16384,65]{1,0:T(8,128)(2,1)}, u32[]{:S(2)}) copy-start(bf16[16384,65]{1,0:T(8,128)(2,1)} %get-tuple-element.387) | copy-start | bytes 6389764 | tf_op jit(solution)/shard_map/while
  231.0 91.8 %copy-start = (bf16[16384,65]{1,0:T(8,128)(2,1)S(1)}, bf16[16384,65]{1,0:T(8,128)(2,1)}, u32[]{:S(2)}) copy-start(bf16[16384,65]{1,0:T(8,128)(2,1)} %get-tuple-element.387) | copy-start | bytes 6389764 | tf_op jit(solution)/shard_map/while
  334.9 91.8 %copy-start = (bf16[16384,65]{1,0:T(8,128)(2,1)S(1)}, bf16[16384,65]{1,0:T(8,128)(2,1)}, u32[]{:S(2)}) copy-start(bf16[16384,65]{1,0:T(8,128)(2,1)} %get-tuple-element.387) | copy-start | bytes 6389764 | tf_op jit(solution)/shard_map/while
  440.0 505.4 %reduce-scatter.2.cloned.1.call-start = ((), (), s32[]{:S(2)}) async-start(), calls=%async_computation.2 | async-start | bytes 5898240 | tf_op jit(solution)/shard_map/reduce_scatter | solution.py:94
  478.4 466.9 %copy-start.1 = (bf16[16384,64]{0,1:T(8,128)(2,1)S(1)}, bf16[16384,64]{0,1:T(8,128)(2,1)}, u32[]{:S(2)}) copy-start(bf16[16384,64]{0,1:T(8,128)(2,1)} %param.11) | copy-start | bytes 6291460
  860.0 188.5 %all-gather.2.cloned.1.call-start = ((), (), s32[]{:S(2)}) async-start(), calls=%async_computation.3 | async-start | bytes 5242880 | tf_op jit(solution)/shard_map/all_gather | solution.py:106
Sparse Core Ops, SparseCore 0:
  440.1 36.1 all-reduce.2
  860.1 85.2 reduce-scatter.1
  947.9 82.4 all-gather.1
where the time goes:
time: 1060 us
  matrix products  422 us (40%)
  other arithmetic  394 us (37%)
  waiting for transfers between devices  122 us (12%)
  blocking collectives  77.9 us (7%)
  local copies, waits for them, and re-layouts  29.7 us (3%)
  between operations  13.9 us (1%)
    dot_general x4, matrix products, add_block(): lax.dot_general(tab, block_mixed, (((0,), (0,)), ((), ())), preferred_ele...  378 us
    dot_general x4, other arithmetic, one_block(): jnp.dot(table_block(block_seeds, first, nfeat), stacked, preferred_elemen...  367 us
    reduce_scatter x1, waiting for transfers between devices, local(): lax.psum_scatter(partial_total, 'rows', scatter_dimension=0, tiled=True)  85.3 us
    psum x1, blocking collectives, local(): core, square, proj = lax.psum((core, square, proj), ('rows', 'sec', 'sub'))  64.8 us
    psum x1, waiting for transfers between devices, local(): margins = lax.psum(local_margins, ('sec', 'sub'))  36.3 us
    dot_general x4, matrix products, one_block(): jnp.dot(table_block(block_seeds, first, nfeat), stacked, preferred_elemen...  35.3 us
  transfers between devices with their start and end apart: 3, of which 2 were waited for; matrix products, arithmetic and copies ran while one was open for 2% of the time, Pallas kernels for 0%

commit v1 on v0

--- a/solution.py
+++ b/solution.py
@@ -88,7 +88,8 @@
     first = lax.axis_index(("sec", "sub")) * nfeat
     stacked = jnp.concatenate([weights.astype(jnp.bfloat16)[:, None], sketch], axis=1)
     local_margins = margin_rows(row_seeds, first, stacked)
-    margins = lax.psum(local_margins, ("sec", "sub"))
+    partial = lax.psum(local_margins, "sub")
+    margins = lax.psum(partial, "sec")
     mixed = weigh(margins, labels)
     partial_total = accumulate(row_seeds, mixed, first, nfeat)
     piece = lax.psum_scatter(partial_total, "rows", scatter_dimension=0, tiled=True)

time: 1060 us -> 1080 us (1.019)
  waiting for transfers between devices: 122 us -> 141 us
    psum x1 -> x2, waiting for transfers between devices: 36.3 us -> 55.2 us  [the longest x1 33.6 us: local(): margins = lax.psum(partial, 'sec')]
  transfers between devices with their start and end apart: 3 -> 4, of which waited for: 2 -> 3; matrix products, arithmetic and copies ran while one was open for 2% -> 2% of each run, Pallas kernels for 0% -> 0%
where the time goes in v1:
time: 1080 us
  matrix products  422 us (39%)
  other arithmetic  394 us (36%)
  waiting for transfers between devices  141 us (13%)
  blocking collectives  78 us (7%)
  local copies, waits for them, and re-layouts  29.7 us (3%)
  between operations  13.9 us (1%)
    dot_general x4, matrix products, add_block(): lax.dot_general(tab, block_mixed, (((0,), (0,)), ((), ())), preferred_ele...  378 us
    dot_general x4, other arithmetic, one_block(): jnp.dot(table_block(block_seeds, first, nfeat), stacked, preferred_elemen...  367 us
    reduce_scatter x1, waiting for transfers between devices, local(): lax.psum_scatter(partial_total, 'rows', scatter_dimension=0, tiled=True)  85.4 us
    psum x1, blocking collectives, local(): core, square, proj = lax.psum((core, square, proj), ('rows', 'sec', 'sub'))  64.8 us
    dot_general x4, matrix products, one_block(): jnp.dot(table_block(block_seeds, first, nfeat), stacked, preferred_elemen...  35.3 us
    psum x1, waiting for transfers between devices, local(): margins = lax.psum(partial, 'sec')  33.6 us
    psum x1, waiting for transfers between devices, local(): partial = lax.psum(local_margins, 'sub')  21.6 us
  transfers between devices with their start and end apart: 4, of which 3 were waited for; matrix products, arithmetic and copies ran while one was open for 2% of the time, Pallas kernels for 0%

profile of v1, /device:TPU:0, one launch (start us, length us, event | category | flops | bytes accessed | tf_op | source)
XLA Modules:
  0.0 1079.3 jit_solution(16345287337990603157)
XLA Ops:
  7.2 0.0 all-reduce.4.cloned.1.call-start
  7.2 0.8 convert_element_type.47
  8.1 3.8 broadcast_in_dim.39
  11.9 4.7 copy.29
  16.7 0.7 reshape.76
  17.4 5.9 pad_maximum_fusion
  23.3 415.5 %while.30 = (s32[]{:T(128)}, f32[4,512,65]{1,0,2:T(4,128)S(1)}, s32[4,512]{1,0:T(4,128)S(1)}, s32[]{:T(128)}, bf16[16384,65]{1,0:T(8,128)(2,1)}, /*index=5*/s32[]{:T(128)}, s32[]{:T(128)}) while((s32[]{:T(128)}, f32[4,512,65]{1,0,2:T(4,128)S(1)}, s32[4,512]{1,0:T(4,128)S(1)}, s32[]{:T(128)}, bf16[16384,65]{1,0:T(8,128)(2,1)}, ...), condition=%wide.region_1.2_spmd, body=%wide.region_0.1_spmd.sunk | while | flops 1459752448 | bytes 45011060 | solution.py:36
  23.4 91.7 %fusion.121 = bf16[512,16384]{1,0:T(8,128)(2,1)} fusion(s32[16384]{0:T(1024)S(1)} %add_select_fusion.18, s32[512]{0:T(512)S(1)} %add_select_fusion.19), kind=kLoop, calls=%fused_computation.18.clone.clone.clone.clone.1.clone.1 | loop fusion | flops 369098752 | bytes 16844800 | tf_op jit(solution)/shard_map/while/body/eval_jaxpr/dot_general | solution.py:32
  115.0 8.8 fusion.122
  123.9 0.1 copy.44
  124.0 3.1 dynamic_update_slice.9
  127.3 91.7 %fusion.121 = bf16[512,16384]{1,0:T(8,128)(2,1)} fusion(s32[16384]{0:T(1024)S(1)} %add_select_fusion.18, s32[512]{0:T(512)S(1)} %add_select_fusion.19), kind=kLoop, calls=%fused_computation.18.clone.clone.clone.clone.1.clone.1 | loop fusion | flops 369098752 | bytes 16844800 | tf_op jit(solution)/shard_map/while/body/eval_jaxpr/dot_general | solution.py:32
  218.9 8.8 fusion.122
  227.7 0.1 copy.44
  227.9 3.1 dynamic_update_slice.9
  231.1 91.7 %fusion.121 = bf16[512,16384]{1,0:T(8,128)(2,1)} fusion(s32[16384]{0:T(1024)S(1)} %add_select_fusion.18, s32[512]{0:T(512)S(1)} %add_select_fusion.19), kind=kLoop, calls=%fused_computation.18.clone.clone.clone.clone.1.clone.1 | loop fusion | flops 369098752 | bytes 16844800 | tf_op jit(solution)/shard_map/while/body/eval_jaxpr/dot_general | solution.py:32
  322.8 8.8 fusion.122
  331.6 0.1 copy.44
  331.8 3.1 dynamic_update_slice.9
  335.0 91.7 %fusion.121 = bf16[512,16384]{1,0:T(8,128)(2,1)} fusion(s32[16384]{0:T(1024)S(1)} %add_select_fusion.18, s32[512]{0:T(512)S(1)} %add_select_fusion.19), kind=kLoop, calls=%fused_computation.18.clone.clone.clone.clone.1.clone.1 | loop fusion | flops 369098752 | bytes 16844800 | tf_op jit(solution)/shard_map/while/body/eval_jaxpr/dot_general | solution.py:32
  426.7 8.8 fusion.122
  435.5 0.1 copy.44
  435.7 3.1 dynamic_update_slice.9
  438.8 0.1 pad.4
  438.9 1.0 copy.42
  440.0 0.0 all-reduce.6.cloned.1.call-start
  440.0 21.6 %all-reduce.4.cloned.1.call-done = f32[2048,65]{0,1:T(8,128)} async-done(((f32[2048,65]{0,1:T(8,128)}), f32[2048,65]{0,1:T(8,128)}) %all-reduce.4.cloned.1.call-update) | async-done | bytes 532496 | tf_op jit(solution)/shard_map/psum | solution.py:91
  461.7 0.0 reduce-scatter.2.cloned.1.call-start
  461.7 33.6 %all-reduce.6.cloned.1.call-done = f32[2048,65]{0,1:T(8,128)} async-done(((f32[2048,65]{0,1:T(8,128)}), f32[2048,65]{0,1:T(8,128)}) %all-reduce.6.cloned.1.call-update) | async-done | bytes 532496 | tf_op jit(solution)/shard_map/psum | solution.py:92
  495.3 0.9 subtract_multiply_fusion.1
  496.2 1.1 fusion.77
  497.4 0.1 pad_maximum_fusion.1
  497.4 381.5 %while.31 = (s32[]{:T(128)}, f32[16384,65]{0,1:T(8,128)}, s32[2048]{0:T(1024)}, s32[]{:T(128)}, bf16[2048,65]{0,1:T(8,128)(2,1)S(1)}, /*index=5*/s32[]{:T(128)}, s32[]{:T(128)}, s32[]{:T(128)}, s32[]{:T(128)}) while((s32[]{:T(128)}, f32[16384,65]{0,1:T(8,128)}, s32[2048]{0:T(1024)}, s32[]{:T(128)}, bf16[2048,65]{0,1:T(8,128)(2,1)S(1)}, ...), condition=%wide.region_5.6_spmd.clone, body=%wide.region_4.5_spmd.clone.sunk | while | flops 1461882368 | bytes 8730785 | solution.py:52
  497.6 0.9 add_select_fusion.21
  498.6 93.6 %convolution_add_fusion.2 = f32[16384,65]{0,1:T(8,128)} fusion(s32[16384]{0:T(1024)S(1)} %add_select_fusion.20, s32[512]{0:T(512)S(1)} %add_select_fusion.21, f32[16384,65]{0,1:T(8,128)} %get-tuple-element.400, pred[]{:T(512)S(6)} %compare.19, bf16[2048,65]{0,1:T(8,128)(2,1)S(1)} %get-tuple-element.412, s32[]{:T(128)S(6)} %select_n.397), kind=kOutput, calls=%fused_computation.70.clone.3 | convolution fusion | flops 1461747712 | bytes 8660997 | tf_op jit(solution)/shard_map/while/body/eval_jaxpr/dot_general | solution.py:48
  592.1 0.8 add_select_fusion.21
  593.0 94.8 %convolution_add_fusion.2 = f32[16384,65]{0,1:T(8,128)} fusion(s32[16384]{0:T(1024)S(1)} %add_select_fusion.20, s32[512]{0:T(512)S(1)} %add_select_fusion.21, f32[16384,65]{0,1:T(8,128)} %get-tuple-element.400, pred[]{:T(512)S(6)} %compare.19, bf16[2048,65]{0,1:T(8,128)(2,1)S(1)} %get-tuple-element.412, s32[]{:T(128)S(6)} %select_n.397), kind=kOutput, calls=%fused_computation.70.clone.3 | convolution fusion | flops 1461747712 | bytes 8660997 | tf_op jit(solution)/shard_map/while/body/eval_jaxpr/dot_general | solution.py:48
  687.7 0.8 add_select_fusion.21
  688.6 94.8 %convolution_add_fusion.2 = f32[16384,65]{0,1:T(8,128)} fusion(s32[16384]{0:T(1024)S(1)} %add_select_fusion.20, s32[512]{0:T(512)S(1)} %add_select_fusion.21, f32[16384,65]{0,1:T(8,128)} %get-tuple-element.400, pred[]{:T(512)S(6)} %compare.19, bf16[2048,65]{0,1:T(8,128)(2,1)S(1)} %get-tuple-element.412, s32[]{:T(128)S(6)} %select_n.397), kind=kOutput, calls=%fused_computation.70.clone.3 | convolution fusion | flops 1461747712 | bytes 8660997 | tf_op jit(solution)/shard_map/while/body/eval_jaxpr/dot_general | solution.py:48
  783.3 0.8 add_select_fusion.21
  784.2 94.8 %convolution_add_fusion.2 = f32[16384,65]{0,1:T(8,128)} fusion(s32[16384]{0:T(1024)S(1)} %add_select_fusion.20, s32[512]{0:T(512)S(1)} %add_select_fusion.21, f32[16384,65]{0,1:T(8,128)} %get-tuple-element.400, pred[]{:T(512)S(6)} %compare.19, bf16[2048,65]{0,1:T(8,128)(2,1)S(1)} %get-tuple-element.412, s32[]{:T(128)S(6)} %select_n.397), kind=kOutput, calls=%fused_computation.70.clone.3 | convolution fusion | flops 1461747712 | bytes 8660997 | tf_op jit(solution)/shard_map/while/body/eval_jaxpr/dot_general | solution.py:48
  878.9 0.0 reduce-scatter.2.cloned.1.call-update
  879.0 0.0 all-gather.2.cloned.1.call-start
  879.0 85.4 %reduce-scatter.2.cloned.1.call-done = f32[4096,65]{0,1:T(8,128)} async-done(((f32[16384,65]{0,1:T(8,128)}), f32[4096,65]{0,1:T(8,128)}) %reduce-scatter.2.cloned.1.call-update) | async-done | bytes 1064976 | tf_op jit(solution)/shard_map/reduce_scatter | solution.py:95
  964.4 2.4 slice_add_fusion
  966.8 0.0 all-gather.2.cloned.1.call-update
  966.8 0.9 slice.32
  967.7 0.7 multiply_add_fusion.1
  968.5 2.2 convolution_bitcast_fusion
  970.6 1.8 fusion.78
  972.5 2.6 fusion.91
  975.1 64.8 %all-reduce = (f32[64,64]{0,1:T(8,128)S(1)}, f32[64,64]{0,1:T(8,128)S(1)}, f32[64]{0:T(128)S(1)}) all-reduce(f32[64,64]{0,1:T(8,128)S(1)} %fusion.91, f32[64,64]{0,1:T(8,128)S(1)} %fusion.78, f32[64]{0:T(128)S(1)} %convolution_bitcast_fusion), channel_id=1, replica_groups=mesh['group'=2,'rows'=4,'sec'=2,'sub'=2] {'rows','sec','sub'}, use_global_device_ids=true, to_apply=%region_8.9 | all-reduce | flops 8256 | bytes 66048 | tf_op jit(solution)/shard_map/psum | solution.py:103
  1039.9 0.1 copy.34
  1040.0 0.1 copy.35
  1040.1 5.8 cholesky.16
  1045.9 0.6 compare_reduce_fusion
  1046.6 0.7 fusion.80
  1047.2 4.9 custom-call.8
  1052.1 0.2 convolution_bitcast_fusion.2
  1052.3 0.2 convolution_bitcast_fusion.1
  1052.5 1.9 fusion.92
  1054.4 13.2 %all_gather.6 = f32[16384]{0:T(1024)S(1)} all-gather(f32[4096]{0:T(1024)S(1)} %subtract_multiply_fusion), channel_id=1, replica_groups=mesh['group'=2,'rows'=4,'sec'=2,'sub'=2] {'rows'}, dimensions={0}, use_global_device_ids=true | all-gather | bytes 81920 | tf_op jit(solution)/shard_map/all_gather | solution.py:106
  1067.6 0.6 copy.62
  1068.2 4.5 copy.63
  (40 shorter events, 0.6 us)
Async XLA Ops:
  7.2 454.5 %all-reduce.4.cloned.1.call-start = ((), (), s32[]{:S(2)}) async-start(), calls=%async_computation.1 | async-start | bytes 1179648 | tf_op jit(solution)/shard_map/psum | solution.py:91
  23.3 472.9 %copy-start.2 = (s32[2048]{0:T(1024)S(1)}, s32[2048]{0:T(1024)}, u32[]{:S(2)}) copy-start(s32[2048]{0:T(1024)} %param.9) | copy-start | bytes 24580
  23.3 91.7 %copy-start = (bf16[16384,65]{1,0:T(8,128)(2,1)S(1)}, bf16[16384,65]{1,0:T(8,128)(2,1)}, u32[]{:S(2)}) copy-start(bf16[16384,65]{1,0:T(8,128)(2,1)} %get-tuple-element.387) | copy-start | bytes 6389764 | tf_op jit(solution)/shard_map/while
  127.2 91.8 %copy-start = (bf16[16384,65]{1,0:T(8,128)(2,1)S(1)}, bf16[16384,65]{1,0:T(8,128)(2,1)}, u32[]{:S(2)}) copy-start(bf16[16384,65]{1,0:T(8,128)(2,1)} %get-tuple-element.387) | copy-start | bytes 6389764 | tf_op jit(solution)/shard_map/while
  231.0 91.8 %copy-start = (bf16[16384,65]{1,0:T(8,128)(2,1)S(1)}, bf16[16384,65]{1,0:T(8,128)(2,1)}, u32[]{:S(2)}) copy-start(bf16[16384,65]{1,0:T(8,128)(2,1)} %get-tuple-element.387) | copy-start | bytes 6389764 | tf_op jit(solution)/shard_map/while
  334.9 91.8 %copy-start = (bf16[16384,65]{1,0:T(8,128)(2,1)S(1)}, bf16[16384,65]{1,0:T(8,128)(2,1)}, u32[]{:S(2)}) copy-start(bf16[16384,65]{1,0:T(8,128)(2,1)} %get-tuple-element.387) | copy-start | bytes 6389764 | tf_op jit(solution)/shard_map/while
  440.0 55.4 %all-reduce.6.cloned.1.call-start = ((), (), s32[]{:S(2)}) async-start(), calls=%async_computation.2 | async-start | bytes 1179648 | tf_op jit(solution)/shard_map/psum | solution.py:92
  461.7 502.7 %reduce-scatter.2.cloned.1.call-start = ((), (), s32[]{:S(2)}) async-start(), calls=%async_computation.3 | async-start | bytes 5898240 | tf_op jit(solution)/shard_map/reduce_scatter | solution.py:95
  497.4 467.0 %copy-start.1 = (bf16[16384,64]{0,1:T(8,128)(2,1)S(1)}, bf16[16384,64]{0,1:T(8,128)(2,1)}, u32[]{:S(2)}) copy-start(bf16[16384,64]{0,1:T(8,128)(2,1)} %param.11) | copy-start | bytes 6291460
  879.0 188.6 %all-gather.2.cloned.1.call-start = ((), (), s32[]{:S(2)}) async-start(), calls=%async_computation.4 | async-start | bytes 5242880 | tf_op jit(solution)/shard_map/all_gather | solution.py:107
Sparse Core Ops, SparseCore 0:
  440.1 21.5 all-reduce.3
  464.1 31.2 all-reduce.5
  879.1 85.2 reduce-scatter.1
  967.0 82.4 all-gather.1
